TPU v7x, 32 devices: a whole 2x2x4 slice. The times are simulated.
32 devices in a mesh: band: 4 (over x, core), grid: 8 (over z, y).
Axes of the slice: x: 2, y: 2, z: 4, core: 2. Of those that a mesh axis runs over, the one named last changes fastest.
Arguments:
- orbitals: float32 [4, 128, 128, 128], P('band', 'grid'), may hold values from -4 to 10, as said below
- pivots: int32 [4], replicated, may hold values from 0 to 2097151, as said below
- pattern: int32 [4, 4], replicated, may hold values from 0 to 1, as said below
Outputs:
- localized: float32 [4, 128, 128, 128], P('band', 'grid')
- exchange_term: float32 [4, 128, 128, 128], P('band', 'grid')
Inputs may be any that keep to these rules, and one draw needn't show every extreme that they name: Values of the orbitals on the grid; the matrix of their values at the pivots has a Cholesky factorization. `pivots`: distinct flat cell indices; the first and the last cell of the grid are always among them. `pattern`: every diagonal entry is 1; each row holds 1 to 4 ones, some row exactly 4; the matrix holds exactly 8 ones.
All inputs are finite; a program needn't handle non-finite values.
Results may differ from a plain program's by a relative error of at most 0.0003.
Values sent between devices are 32-bit elements; how exact they have to be, the bound alone decides.
A program may use at most 64 MiB of HBM per device.

v0:
```python
import jax
import jax.numpy as jnp
from jax import lax
from jax.sharding import PartitionSpec as P

MOST_PARTNERS = 4
precise = lax.Precision.HIGHEST


def tables(length):
    across = jnp.arange(length, dtype=jnp.int32)
    phases = across[:, None] * across[None, :] % length
    angles = phases.astype(jnp.float32) * (2.0 * jnp.pi / length)
    return (jnp.cos(angles), jnp.sin(angles))


def wrapped(indices, length):
    return jnp.where(indices < length // 2, indices, indices - length)


def coulomb(length, plane_start, plane_count):
    wave_first = wrapped(jnp.arange(length, dtype=jnp.int32), length).astype(jnp.float32)
    wave_second = wrapped(plane_start + jnp.arange(plane_count, dtype=jnp.int32), length).astype(
        jnp.float32
    )
    squared = (
        wave_first[:, None, None] ** 2
        + wave_second[None, :, None] ** 2
        + wave_first[None, None, :] ** 2
    )
    scaling = float(length) ** 1.5
    return jnp.where(squared > 0, 0.25 / (scaling * jnp.maximum(squared, 1.0)), 0.0)


def densities(first_bands, second_bands):
    return (first_bands[:, None] * second_bands[None, :]).reshape((-1,) + first_bands.shape[1:])


def applied(potential, first_bands, second_bands):
    shaped = potential.reshape(
        (first_bands.shape[0], second_bands.shape[0]) + first_bands.shape[1:]
    )
    return jnp.sum(shaped * second_bands[None], axis=1)


def filtered(real_in, imag_in, kernel, cos_table, sin_table):
    real_part = jnp.dot(real_in, cos_table, precision=precise) + jnp.dot(
        imag_in, sin_table, precision=precise
    )
    imag_part = jnp.dot(imag_in, cos_table, precision=precise) - jnp.dot(
        real_in, sin_table, precision=precise
    )
    real_part, imag_part = (
        jnp.einsum("pxyz,yk->pxkz", real_part, cos_table, precision=precise)
        + jnp.einsum("pxyz,yk->pxkz", imag_part, sin_table, precision=precise),
        jnp.einsum("pxyz,yk->pxkz", imag_part, cos_table, precision=precise)
        - jnp.einsum("pxyz,yk->pxkz", real_part, sin_table, precision=precise),
    )
    real_wide = lax.all_to_all(real_part, "grid", split_axis=2, concat_axis=1, tiled=True)
    imag_wide = lax.all_to_all(imag_part, "grid", split_axis=2, concat_axis=1, tiled=True)
    ahead_real = (
        jnp.einsum("pxyz,xk->pkyz", real_wide, cos_table, precision=precise)
        + jnp.einsum("pxyz,xk->pkyz", imag_wide, sin_table, precision=precise)
    ) * kernel
    ahead_imag = (
        jnp.einsum("pxyz,xk->pkyz", imag_wide, cos_table, precision=precise)
        - jnp.einsum("pxyz,xk->pkyz", real_wide, sin_table, precision=precise)
    ) * kernel
    back_real = jnp.einsum("pxyz,xk->pkyz", ahead_real, cos_table, precision=precise) - jnp.einsum(
        "pxyz,xk->pkyz", ahead_imag, sin_table, precision=precise
    )
    back_imag = jnp.einsum("pxyz,xk->pkyz", ahead_imag, cos_table, precision=precise) + jnp.einsum(
        "pxyz,xk->pkyz", ahead_real, sin_table, precision=precise
    )
    real_part = lax.all_to_all(back_real, "grid", split_axis=1, concat_axis=2, tiled=True)
    imag_part = lax.all_to_all(back_imag, "grid", split_axis=1, concat_axis=2, tiled=True)
    real_part, imag_part = (
        jnp.einsum("pxyz,yk->pxkz", real_part, cos_table, precision=precise)
        - jnp.einsum("pxyz,yk->pxkz", imag_part, sin_table, precision=precise),
        jnp.einsum("pxyz,yk->pxkz", imag_part, cos_table, precision=precise)
        + jnp.einsum("pxyz,yk->pxkz", real_part, sin_table, precision=precise),
    )
    out_real = jnp.dot(real_part, cos_table, precision=precise) - jnp.dot(
        imag_part, sin_table, precision=precise
    )
    out_imag = jnp.dot(imag_part, cos_table, precision=precise) + jnp.dot(
        real_part, sin_table, precision=precise
    )
    return (out_real, out_imag)


def twin_potential(first_one, second_one, first_two, second_two, kernel, cos_table, sin_table):
    potential_one, potential_two = filtered(
        densities(first_one, second_one),
        densities(first_two, second_two),
        kernel,
        cos_table,
        sin_table,
    )
    return (
        applied(potential_one, first_one, second_one),
        applied(potential_two, first_two, second_two),
    )


def collect(wanted, portion):
    positions = jnp.arange(portion.shape[0], dtype=jnp.int32)
    chooser = (wanted[:, None] == positions[None, :]).astype(jnp.float32)
    return jnp.einsum("qm,mxyz->qxyz", chooser, portion, precision=precise)


def local(orbitals, pivots, pattern):
    band_dev = orbitals.shape[0]
    slab_planes = orbitals.shape[1]
    length = orbitals.shape[3]
    block_total = pattern.shape[0]
    grid_index = lax.axis_index("grid")
    band_index = lax.axis_index("band")
    cell_count = slab_planes * length * length
    flat_local = orbitals.reshape(band_dev, cell_count)
    local_cell = pivots - grid_index * cell_count
    inside = (local_cell >= 0) & (local_cell < cell_count)
    sampled = jnp.take(flat_local, jnp.clip(local_cell, 0, cell_count - 1), axis=1)
    partial_pick = jnp.where(inside[None, :], sampled, 0.0)
    own_rows = lax.psum(partial_pick, "grid")
    picked = lax.all_gather(own_rows, "band", axis=0, tiled=True)
    gram_matrix = jnp.dot(picked.T, picked, precision=precise)
    factor = jnp.linalg.cholesky(gram_matrix)
    rotation = lax.linalg.triangular_solve(factor, picked.T, left_side=True, lower=True).T
    own_weights = lax.dynamic_slice_in_dim(rotation, band_index * band_dev, band_dev, 0)
    localized = lax.psum_scatter(
        jnp.einsum("bk,bxyz->kxyz", own_weights, orbitals, precision=precise),
        "band",
        scatter_dimension=0,
        tiled=True,
    )
    cos_table, sin_table = tables(length)
    plane_count = length // lax.axis_size("grid")
    kernel = coulomb(length, grid_index * plane_count, plane_count)
    columns = jnp.arange(block_total, dtype=jnp.int32)
    members = jnp.arange(band_dev, dtype=jnp.int32)
    own_row = lax.dynamic_index_in_dim(pattern, band_index, 0, keepdims=False)
    before = jnp.cumsum(own_row) - own_row
    slot_ids = jnp.arange(MOST_PARTNERS, dtype=jnp.int32)
    matches = (own_row[None, :] == 1) & (before[None, :] == slot_ids[:, None])
    partner = jnp.sum(jnp.where(matches, columns[None, :], 0), axis=1)
    present = jnp.any(matches, axis=1)
    wanted = jnp.where(
        present[:, None], partner[:, None] * band_dev + members[None, :], -1
    ).reshape(-1)
    partners = collect(wanted, lax.all_gather(localized, "band", axis=0, tiled=True))
    exchange_term = jnp.zeros_like(localized)
    for couple in range(MOST_PARTNERS // 2):
        first_rows = partners[2 * couple * band_dev : (2 * couple + 1) * band_dev]
        second_rows = partners[(2 * couple + 1) * band_dev : (2 * couple + 2) * band_dev]
        term_one, term_two = twin_potential(
            localized, first_rows, localized, second_rows, kernel, cos_table, sin_table
        )
        exchange_term = exchange_term + term_one + term_two
    return (localized, exchange_term)


def solution(mesh):
    return jax.shard_map(
        local,
        mesh=mesh,
        in_specs=(P("band", "grid", None, None), P(), P()),
        out_specs=(P("band", "grid", None, None), P("band", "grid", None, None)),
        check_vma=False,
    )
```

profile of v0, /device:TPU:0, one launch (start us, length us, event | category | flops | bytes accessed | tf_op | source)
XLA Modules:
  0.0 410.0 jit_solution(14240325148722384985)
XLA Ops:
  10.0 23.1 %psum.7 = f32[1,4]{1,0:T(1,128)S(1)} all-reduce(f32[1,4]{1,0:T(1,128)S(1)} %fusion.210), channel_id=1, replica_groups=mesh['band'=4,'grid'=8] {'grid'}, use_global_device_ids=true, to_apply=%region_0.1 | all-reduce | flops 4 | bytes 32 | tf_op jit(solution)/shard_map/psum | solution.py:125
  33.1 5.0 %all-gather = f32[4,1,4]{2,1,0:T(1,128)S(1)} all-gather(f32[1,1,4]{2,1,0:T(1,128)S(1)} %bitcast.338), channel_id=1, replica_groups=mesh['band'=4,'grid'=8] {'band'}, dimensions={0}, use_global_device_ids=true | all-gather | bytes 80 | tf_op jit(solution)/shard_map/all_gather | solution.py:126
  40.6 3.8 broadcast_multiply_fusion
  44.4 41.9 %reduce-scatter.2.cloned.1.call-done = f32[1,16,128,128]{3,2,1,0:T(8,128)} async-done(((f32[4,16,128,128]{3,2,1,0:T(8,128)}), f32[1,16,128,128]{3,2,1,0:T(8,128)}) %reduce-scatter.2.cloned.1.call-update) | async-done | bytes 1048592 | tf_op jit(solution)/shard_map/reduce_scatter | solution.py:131
  87.5 35.6 %all-gather.3.cloned.1.call-done = f32[4,16,128,128]{3,2,1,0:T(8,128)} async-done(((f32[1,16,128,128]{3,2,1,0:T(8,128)}), f32[4,16,128,128]{3,2,1,0:T(8,128)}) %all-gather.3.cloned.1.call-update) | async-done | bytes 4194320 | tf_op jit(solution)/shard_map/all_gather | solution.py:151
  123.0 8.5 %fusion = f32[4,16,128,128]{3,0,2,1:T(4,128)S(1)} fusion(f32[4,16,128,128]{3,2,1,0:T(8,128)} %all-gather.3.cloned.1.call-done, s32[4]{0:T(128)S(1)} %broadcast_select_fusion), kind=kOutput, calls=%fused_computation.1 | convolution fusion | flops 50331664 | bytes 8388624 | tf_op jit(solution)/shard_map/qm,mxyz->qxyz/dot_general | solution.py:109
  131.6 3.6 slice_multiply_fusion.3
  145.2 5.8 %all-to-all-start.4 = ((f32[1,16,128,128]{3,1,0,2:T(8,128)}), f32[1,16,128,128]{3,1,0,2:T(8,128)}, u32[]{:S(2)}, u32[]{:S(2)}) async-start(f32[1,16,128,128]{3,1,0,2:T(8,128)} %copy.182), calls=%async_computation.5 | async-start | bytes 2097152 | tf_op jit(solution)/shard_map/all_to_all | solution.py:59
  152.3 2.5 fusion.8
  154.8 1.6 copy.187
  156.4 20.8 %all-to-all-done.4 = f32[1,16,128,128]{3,1,0,2:T(8,128)} async-done(((f32[1,16,128,128]{3,1,0,2:T(8,128)}), f32[1,16,128,128]{3,1,0,2:T(8,128)}, u32[]{:S(2)}, u32[]{:S(2)}) %all-to-all-start.4) | async-done | bytes 1048608 | tf_op jit(solution)/shard_map/all_to_all | solution.py:59
  177.2 4.2 %all-to-all-start.5 = ((f32[1,16,128,128]{3,1,0,2:T(8,128)}), f32[1,16,128,128]{3,1,0,2:T(8,128)}, u32[]{:S(2)}, u32[]{:S(2)}) async-start(f32[1,16,128,128]{3,1,0,2:T(8,128)} %copy.187), calls=%async_computation.6 | async-start | bytes 2097152 | tf_op jit(solution)/shard_map/all_to_all | solution.py:60
  190.5 16.5 %all-to-all-done.5 = f32[1,16,128,128]{3,1,0,2:T(8,128)} async-done(((f32[1,16,128,128]{3,1,0,2:T(8,128)}), f32[1,16,128,128]{3,1,0,2:T(8,128)}, u32[]{:S(2)}, u32[]{:S(2)}) %all-to-all-start.5) | async-done | bytes 1048608 | tf_op jit(solution)/shard_map/all_to_all | solution.py:60
  207.1 4.0 all-to-all-start.1
  213.7 1.6 copy.156
  215.3 21.6 %all-to-all-done.1 = f32[1,16,128,128]{3,1,0,2:T(8,128)S(1)} async-done(((f32[1,16,128,128]{3,1,0,2:T(8,128)}), f32[1,16,128,128]{3,1,0,2:T(8,128)S(1)}, u32[]{:S(2)}, u32[]{:S(2)}) %all-to-all-start.1) | async-done | bytes 1048608 | tf_op jit(solution)/shard_map/all_to_all | solution.py:60
  236.8 3.6 all-to-all-start
  251.4 1.6 copy.194
  253.0 13.5 %all-to-all-done = f32[1,16,128,128]{3,1,0,2:T(8,128)S(1)} async-done(((f32[1,16,128,128]{3,1,0,2:T(8,128)}), f32[1,16,128,128]{3,1,0,2:T(8,128)S(1)}, u32[]{:S(2)}, u32[]{:S(2)}) %all-to-all-start) | async-done | bytes 1048608 | tf_op jit(solution)/shard_map/all_to_all | solution.py:59
  267.4 3.8 all-to-all-start.6
  273.8 1.6 copy.199
  275.4 21.8 %all-to-all-done.6 = f32[1,128,16,128]{3,2,0,1:T(8,128)S(1)} async-done(((f32[1,128,16,128]{3,2,0,1:T(8,128)}), f32[1,128,16,128]{3,2,0,1:T(8,128)S(1)}, u32[]{:S(2)}, u32[]{:S(2)}) %all-to-all-start.6) | async-done | bytes 1048608 | tf_op jit(solution)/shard_map/all_to_all | solution.py:75
  297.2 4.2 %all-to-all-start.7 = ((f32[1,128,16,128]{3,2,0,1:T(8,128)}), f32[1,128,16,128]{3,2,0,1:T(8,128)}, u32[]{:S(2)}, u32[]{:S(2)}) async-start(f32[1,128,16,128]{3,2,0,1:T(8,128)} %copy.199), calls=%async_computation.8 | async-start | bytes 2097152 | tf_op jit(solution)/shard_map/all_to_all | solution.py:76
  309.8 1.6 copy.173
  311.4 15.6 %all-to-all-done.7 = f32[1,128,16,128]{3,2,0,1:T(8,128)} async-done(((f32[1,128,16,128]{3,2,0,1:T(8,128)}), f32[1,128,16,128]{3,2,0,1:T(8,128)}, u32[]{:S(2)}, u32[]{:S(2)}) %all-to-all-start.7) | async-done | bytes 1048608 | tf_op jit(solution)/shard_map/all_to_all | solution.py:76
  327.1 4.6 %all-to-all-start.3 = ((f32[1,128,16,128]{3,2,0,1:T(8,128)}), f32[1,128,16,128]{3,2,0,1:T(8,128)}, u32[]{:S(2)}, u32[]{:S(2)}) async-start(f32[1,128,16,128]{3,2,0,1:T(8,128)} %copy.173), calls=%async_computation.4 | async-start | bytes 2097152 | tf_op jit(solution)/shard_map/all_to_all | solution.py:76
  334.3 1.6 copy.168
  337.3 2.3 fusion.48
  339.6 17.5 %all-to-all-done.3 = f32[1,128,16,128]{3,2,0,1:T(8,128)} async-done(((f32[1,128,16,128]{3,2,0,1:T(8,128)}), f32[1,128,16,128]{3,2,0,1:T(8,128)}, u32[]{:S(2)}, u32[]{:S(2)}) %all-to-all-start.3) | async-done | bytes 1048608 | tf_op jit(solution)/shard_map/all_to_all | solution.py:76
  357.1 4.2 %all-to-all-start.2 = ((f32[1,128,16,128]{3,2,0,1:T(8,128)}), f32[1,128,16,128]{3,2,0,1:T(8,128)}, u32[]{:S(2)}, u32[]{:S(2)}) async-start(f32[1,128,16,128]{3,2,0,1:T(8,128)} %copy.168), calls=%async_computation.3 | async-start | bytes 2097152 | tf_op jit(solution)/shard_map/all_to_all | solution.py:75
  371.6 15.2 %all-to-all-done.2 = f32[1,128,16,128]{3,2,0,1:T(8,128)} async-done(((f32[1,128,16,128]{3,2,0,1:T(8,128)}), f32[1,128,16,128]{3,2,0,1:T(8,128)}, u32[]{:S(2)}, u32[]{:S(2)}) %all-to-all-start.2) | async-done | bytes 1048608 | tf_op jit(solution)/shard_map/all_to_all | solution.py:75
  398.4 4.5 %multiply_add_fusion = f32[1,16,128,128]{3,0,2,1:T(1,128)} fusion(f32[1,16,128,128]{3,0,2,1:T(1,128)S(1)} %bitcast.318, f32[1,16,128,128]{3,0,2,1:T(1,128)S(1)} %bitcast.317, f32[1,16,128,128]{3,0,2,1:T(1,128)S(1)} %bitcast.319, f32[1,16,128,128]{3,0,2,1:T(1,128)S(1)} %bitcast.320, f32[4,16,128,128]{3,0,2,1:T(4,128)S(1)} %copy-done.1), kind=kLoop, calls=%fused_computation.49 | loop fusion | flops 1835008 | bytes 9437184 | tf_op jit(solution)/shard_map/add | solution.py:159
  (101 shorter events, 77.8 us)
Async XLA Ops:
  7.2 79.1 %reduce-scatter.2.cloned.1.call-start = ((), (), s32[]{:S(2)}) async-start(), calls=%async_computation.9 | async-start | bytes 5242880 | tf_op jit(solution)/shard_map/reduce_scatter | solution.py:131
  44.4 78.6 %all-gather.3.cloned.1.call-start = ((), (), s32[]{:S(2)}) async-start(), calls=%async_computation.10 | async-start | bytes 5242880 | tf_op jit(solution)/shard_map/all_gather | solution.py:151
  87.5 44.1 %copy-start.3 = (f32[1,16,128,128]{3,2,1,0:T(8,128)S(1)}, f32[1,16,128,128]{3,2,1,0:T(8,128)}, u32[]{:S(2)}) copy-start(f32[1,16,128,128]{3,2,1,0:T(8,128)} %reduce-scatter.2.cloned.1.call-done) | copy-start | bytes 3145732
  131.6 3.6 copy-start
  140.1 1.0 copy-start.2
  145.2 32.0 %all-to-all-start.4 = ((f32[1,16,128,128]{3,1,0,2:T(8,128)}), f32[1,16,128,128]{3,1,0,2:T(8,128)}, u32[]{:S(2)}, u32[]{:S(2)}) async-start(f32[1,16,128,128]{3,1,0,2:T(8,128)} %copy.182), calls=%async_computation.5 | async-start | bytes 2097152 | tf_op jit(solution)/shard_map/all_to_all | solution.py:59
  177.2 29.9 %all-to-all-start.5 = ((f32[1,16,128,128]{3,1,0,2:T(8,128)}), f32[1,16,128,128]{3,1,0,2:T(8,128)}, u32[]{:S(2)}, u32[]{:S(2)}) async-start(f32[1,16,128,128]{3,1,0,2:T(8,128)} %copy.187), calls=%async_computation.6 | async-start | bytes 2097152 | tf_op jit(solution)/shard_map/all_to_all | solution.py:60
  207.1 29.7 %all-to-all-start.1 = ((f32[1,16,128,128]{3,1,0,2:T(8,128)}), f32[1,16,128,128]{3,1,0,2:T(8,128)S(1)}, u32[]{:S(2)}, u32[]{:S(2)}) async-start(f32[1,16,128,128]{3,1,0,2:T(8,128)} %copy.161), calls=%async_computation.2 | async-start | bytes 2097152 | tf_op jit(solution)/shard_map/all_to_all | solution.py:60
  236.8 7.7 %copy-start.5 = (f32[1,16,128,128]{3,1,0,2:T(8,128)}, f32[1,16,128,128]{3,1,0,2:T(8,128)S(1)}, u32[]{:S(2)}) copy-start(f32[1,16,128,128]{3,1,0,2:T(8,128)S(1)} %all-to-all-done.1) | copy-start | bytes 3145732
  236.8 29.6 %all-to-all-start = ((f32[1,16,128,128]{3,1,0,2:T(8,128)}), f32[1,16,128,128]{3,1,0,2:T(8,128)S(1)}, u32[]{:S(2)}, u32[]{:S(2)}) async-start(f32[1,16,128,128]{3,1,0,2:T(8,128)} %copy.156), calls=%async_computation.1 | async-start | bytes 2097152 | tf_op jit(solution)/shard_map/all_to_all | solution.py:59
  266.4 1.0 copy-start.7
  267.4 29.8 %all-to-all-start.6 = ((f32[1,128,16,128]{3,2,0,1:T(8,128)}), f32[1,128,16,128]{3,2,0,1:T(8,128)S(1)}, u32[]{:S(2)}, u32[]{:S(2)}) async-start(f32[1,128,16,128]{3,2,0,1:T(8,128)} %copy.194), calls=%async_computation.7 | async-start | bytes 2097152 | tf_op jit(solution)/shard_map/all_to_all | solution.py:75
  272.5 28.9 %copy-start.6 = (f32[1,16,128,128]{3,1,0,2:T(8,128)S(1)}, f32[1,16,128,128]{3,1,0,2:T(8,128)}, u32[]{:S(2)}) copy-start(f32[1,16,128,128]{3,1,0,2:T(8,128)} %copy-done.5) | copy-start | bytes 3145732
  273.8 27.7 %copy-start.8 = (f32[1,16,128,128]{3,1,0,2:T(8,128)S(1)}, f32[1,16,128,128]{3,1,0,2:T(8,128)}, u32[]{:S(2)}) copy-start(f32[1,16,128,128]{3,1,0,2:T(8,128)} %copy-done.7) | copy-start | bytes 3145732
  297.2 29.9 %all-to-all-start.7 = ((f32[1,128,16,128]{3,2,0,1:T(8,128)}), f32[1,128,16,128]{3,2,0,1:T(8,128)}, u32[]{:S(2)}, u32[]{:S(2)}) async-start(f32[1,128,16,128]{3,2,0,1:T(8,128)} %copy.199), calls=%async_computation.8 | async-start | bytes 2097152 | tf_op jit(solution)/shard_map/all_to_all | solution.py:76
  327.1 30.1 %all-to-all-start.3 = ((f32[1,128,16,128]{3,2,0,1:T(8,128)}), f32[1,128,16,128]{3,2,0,1:T(8,128)}, u32[]{:S(2)}, u32[]{:S(2)}) async-start(f32[1,128,16,128]{3,2,0,1:T(8,128)} %copy.173), calls=%async_computation.4 | async-start | bytes 2097152 | tf_op jit(solution)/shard_map/all_to_all | solution.py:76
  357.1 29.7 %all-to-all-start.2 = ((f32[1,128,16,128]{3,2,0,1:T(8,128)}), f32[1,128,16,128]{3,2,0,1:T(8,128)}, u32[]{:S(2)}, u32[]{:S(2)}) async-start(f32[1,128,16,128]{3,2,0,1:T(8,128)} %copy.168), calls=%async_computation.3 | async-start | bytes 2097152 | tf_op jit(solution)/shard_map/all_to_all | solution.py:75
  362.7 4.0 copy-start.4
  394.7 3.7 copy-start.1
Sparse Core Ops, SparseCore 0:
  44.5 41.7 reduce-scatter.1
  88.5 34.4 all-gather.2
where the time goes:
time: 417 us; the launch traced here: 410 us
  waiting for transfers between devices  220 us (53%)
  matrix products  72.7 us (17%)
  starting transfers between devices  34.7 us (8%)
  blocking collectives  28.1 us (7%)
  local copies, waits for them, and re-layouts  23.3 us (6%)
  other arithmetic  16.4 us (4%)
  between operations  14.9 us (4%)
    reduce_scatter x1, waiting for transfers between devices, local(): lax.psum_scatter(jnp.einsum('bk,bxyz->kxyz', own_weights, orbitals, preci...  41.9 us
    all_to_all x2, waiting for transfers between devices, filtered(): lax.all_to_all(imag_part, 'grid', split_axis=2, concat_axis=1, tiled=True)  38.1 us
    all_to_all x2, waiting for transfers between devices, filtered(): lax.all_to_all(back_real, 'grid', split_axis=1, concat_axis=2, tiled=True)  36.9 us
    all_gather x1, waiting for transfers between devices, local(): lax.all_gather(localized, 'band', axis=0, tiled=True)  35.6 us
    all_to_all x2, waiting for transfers between devices, filtered(): lax.all_to_all(real_part, 'grid', split_axis=2, concat_axis=1, tiled=True)  34.3 us
    all_to_all x2, waiting for transfers between devices, filtered(): lax.all_to_all(back_imag, 'grid', split_axis=1, concat_axis=2, tiled=True)  33.2 us
    psum x1, blocking collectives, local(): own_rows = lax.psum(partial_pick, 'grid')  23.1 us
    all_to_all x2, starting transfers between devices, filtered(): lax.all_to_all(real_part, 'grid', split_axis=2, concat_axis=1, tiled=True)  9.43 us
  transfers between devices with their start and end apart: 10, of which 10 were waited for; matrix products, arithmetic and copies ran while one was open for 16% of the time, Pallas kernels for 0%

commit v1 on v0

--- a/solution.py
+++ b/solution.py
@@ -122,7 +122,7 @@
     inside = (local_cell >= 0) & (local_cell < cell_count)
     sampled = jnp.take(flat_local, jnp.clip(local_cell, 0, cell_count - 1), axis=1)
     partial_pick = jnp.where(inside[None, :], sampled, 0.0)
-    own_rows = lax.psum(partial_pick, "grid")
+    own_rows = jnp.sum(lax.all_gather(partial_pick, "grid"), axis=0)
     picked = lax.all_gather(own_rows, "band", axis=0, tiled=True)
     gram_matrix = jnp.dot(picked.T, picked, precision=precise)
     factor = jnp.linalg.cholesky(gram_matrix)

time: 417 us -> 422 us (1.012)
    unnamed x0 -> x2, blocking collectives: none -> 28.7 us
    psum x1 -> x0, blocking collectives: 23.1 us -> none  [local(): own_rows = lax.psum(partial_pick, 'grid')]
    all_gather x1 -> x0, blocking collectives: 5.03 us -> none  [local(): picked = lax.all_gather(own_rows, 'band', axis=0, tiled=True)]
  transfers between devices with their start and end apart: 10 -> 10, of which waited for: 10 -> 10; matrix products, arithmetic and copies ran while one was open for 16% -> 15% of each run, Pallas kernels for 0% -> 0%
where the time goes in v1:
time: 422 us; the launch traced here: 415 us
  waiting for transfers between devices  220 us (52%)
  matrix products  72.7 us (17%)
  starting transfers between devices  34.7 us (8%)
  blocking collectives  28.7 us (7%)
  local copies, waits for them, and re-layouts  26.2 us (6%)
  other arithmetic  16.5 us (4%)
  between operations  16.2 us (4%)
    reduce_scatter x1, waiting for transfers between devices, local(): lax.psum_scatter(jnp.einsum('bk,bxyz->kxyz', own_weights, orbitals, preci...  42.1 us
    all_to_all x2, waiting for transfers between devices, filtered(): lax.all_to_all(imag_part, 'grid', split_axis=2, concat_axis=1, tiled=True)  38.1 us
    all_to_all x2, waiting for transfers between devices, filtered(): lax.all_to_all(back_real, 'grid', split_axis=1, concat_axis=2, tiled=True)  36.9 us
    all_gather x1, waiting for transfers between devices, local(): lax.all_gather(localized, 'band', axis=0, tiled=True)  35.6 us
    all_to_all x2, waiting for transfers between devices, filtered(): lax.all_to_all(real_part, 'grid', split_axis=2, concat_axis=1, tiled=True)  34.3 us
    all_to_all x2, waiting for transfers between devices, filtered(): lax.all_to_all(back_imag, 'grid', split_axis=1, concat_axis=2, tiled=True)  33.1 us
    unnamed x2, blocking collectives  28.7 us
    all_to_all x2, starting transfers between devices, filtered(): lax.all_to_all(real_part, 'grid', split_axis=2, concat_axis=1, tiled=True)  9.43 us
  transfers between devices with their start and end apart: 10, of which 10 were waited for; matrix products, arithmetic and copies ran while one was open for 15% of the time, Pallas kernels for 0%

profile of v1, /device:TPU:0, one launch (start us, length us, event | category | flops | bytes accessed | tf_op | source)
XLA Modules:
  0.0 415.2 jit_solution(1817917066573318548)
XLA Ops:
  13.8 23.1 %all-reduce = f32[32]{0:T(128)S(1)} all-reduce(f32[32]{0:T(128)S(1)} %fusion.158), channel_id=2, replica_groups=mesh['band'=4,'grid'=8] {'grid'}, use_global_device_ids=true, to_apply=%add | all-reduce | flops 32 | bytes 256
  37.3 5.6 %all-reduce.1 = f32[16]{0:T(128)S(1)} all-reduce(f32[16]{0:T(128)S(1)} %dynamic-update-slice.4), channel_id=3, replica_groups=mesh['band'=4,'grid'=8] {'band'}, use_global_device_ids=true, to_apply=%add.1 | all-reduce | flops 16 | bytes 128
  45.5 3.7 broadcast_multiply_fusion
  49.3 42.1 %reduce-scatter.2.cloned.1.call-done = f32[1,16,128,128]{3,2,1,0:T(8,128)} async-done(((f32[4,16,128,128]{3,2,1,0:T(8,128)}), f32[1,16,128,128]{3,2,1,0:T(8,128)}) %reduce-scatter.2.cloned.1.call-update) | async-done | bytes 1048592 | tf_op jit(solution)/shard_map/reduce_scatter | solution.py:131
  92.6 35.6 %all-gather.4.cloned.1.call-done = f32[4,16,128,128]{3,2,1,0:T(8,128)} async-done(((f32[1,16,128,128]{3,2,1,0:T(8,128)}), f32[4,16,128,128]{3,2,1,0:T(8,128)}) %all-gather.4.cloned.1.call-update) | async-done | bytes 4194320 | tf_op jit(solution)/shard_map/all_gather | solution.py:151
  128.2 8.5 %fusion = f32[4,16,128,128]{3,0,2,1:T(4,128)S(1)} fusion(f32[4,16,128,128]{3,2,1,0:T(8,128)} %all-gather.4.cloned.1.call-done, s32[4]{0:T(128)S(1)} %broadcast_select_fusion), kind=kOutput, calls=%fused_computation.1 | convolution fusion | flops 50331664 | bytes 8388624 | tf_op jit(solution)/shard_map/qm,mxyz->qxyz/dot_general | solution.py:109
  136.7 3.6 slice_multiply_fusion.3
  148.8 1.6 copy.182
  150.4 5.8 %all-to-all-start.4 = ((f32[1,16,128,128]{3,1,0,2:T(8,128)}), f32[1,16,128,128]{3,1,0,2:T(8,128)}, u32[]{:S(2)}, u32[]{:S(2)}) async-start(f32[1,16,128,128]{3,1,0,2:T(8,128)} %copy.182), calls=%async_computation.5 | async-start | bytes 2097152 | tf_op jit(solution)/shard_map/all_to_all | solution.py:59
  157.4 2.5 fusion.8
  161.5 20.8 %all-to-all-done.4 = f32[1,16,128,128]{3,1,0,2:T(8,128)} async-done(((f32[1,16,128,128]{3,1,0,2:T(8,128)}), f32[1,16,128,128]{3,1,0,2:T(8,128)}, u32[]{:S(2)}, u32[]{:S(2)}) %all-to-all-start.4) | async-done | bytes 1048608 | tf_op jit(solution)/shard_map/all_to_all | solution.py:59
  182.4 4.3 %all-to-all-start.5 = ((f32[1,16,128,128]{3,1,0,2:T(8,128)}), f32[1,16,128,128]{3,1,0,2:T(8,128)}, u32[]{:S(2)}, u32[]{:S(2)}) async-start(f32[1,16,128,128]{3,1,0,2:T(8,128)} %copy.187), calls=%async_computation.6 | async-start | bytes 2097152 | tf_op jit(solution)/shard_map/all_to_all | solution.py:60
  194.1 1.6 copy.161
  195.7 16.5 %all-to-all-done.5 = f32[1,16,128,128]{3,1,0,2:T(8,128)} async-done(((f32[1,16,128,128]{3,1,0,2:T(8,128)}), f32[1,16,128,128]{3,1,0,2:T(8,128)}, u32[]{:S(2)}, u32[]{:S(2)}) %all-to-all-start.5) | async-done | bytes 1048608 | tf_op jit(solution)/shard_map/all_to_all | solution.py:60
  212.2 4.0 all-to-all-start.1
  218.8 1.6 copy.156
  220.4 21.6 %all-to-all-done.1 = f32[1,16,128,128]{3,1,0,2:T(8,128)S(1)} async-done(((f32[1,16,128,128]{3,1,0,2:T(8,128)}), f32[1,16,128,128]{3,1,0,2:T(8,128)S(1)}, u32[]{:S(2)}, u32[]{:S(2)}) %all-to-all-start.1) | async-done | bytes 1048608 | tf_op jit(solution)/shard_map/all_to_all | solution.py:60
  242.0 3.6 all-to-all-start
  256.5 1.6 copy.194
  258.1 13.5 %all-to-all-done = f32[1,16,128,128]{3,1,0,2:T(8,128)S(1)} async-done(((f32[1,16,128,128]{3,1,0,2:T(8,128)}), f32[1,16,128,128]{3,1,0,2:T(8,128)S(1)}, u32[]{:S(2)}, u32[]{:S(2)}) %all-to-all-start) | async-done | bytes 1048608 | tf_op jit(solution)/shard_map/all_to_all | solution.py:59
  272.6 3.8 all-to-all-start.6
  280.6 21.8 %all-to-all-done.6 = f32[1,128,16,128]{3,2,0,1:T(8,128)S(1)} async-done(((f32[1,128,16,128]{3,2,0,1:T(8,128)}), f32[1,128,16,128]{3,2,0,1:T(8,128)S(1)}, u32[]{:S(2)}, u32[]{:S(2)}) %all-to-all-start.6) | async-done | bytes 1048608 | tf_op jit(solution)/shard_map/all_to_all | solution.py:75
  302.3 4.2 %all-to-all-start.7 = ((f32[1,128,16,128]{3,2,0,1:T(8,128)}), f32[1,128,16,128]{3,2,0,1:T(8,128)}, u32[]{:S(2)}, u32[]{:S(2)}) async-start(f32[1,128,16,128]{3,2,0,1:T(8,128)} %copy.199), calls=%async_computation.8 | async-start | bytes 2097152 | tf_op jit(solution)/shard_map/all_to_all | solution.py:76
  315.0 1.6 copy.173
  316.6 15.6 %all-to-all-done.7 = f32[1,128,16,128]{3,2,0,1:T(8,128)} async-done(((f32[1,128,16,128]{3,2,0,1:T(8,128)}), f32[1,128,16,128]{3,2,0,1:T(8,128)}, u32[]{:S(2)}, u32[]{:S(2)}) %all-to-all-start.7) | async-done | bytes 1048608 | tf_op jit(solution)/shard_map/all_to_all | solution.py:76
  332.2 4.6 %all-to-all-start.3 = ((f32[1,128,16,128]{3,2,0,1:T(8,128)}), f32[1,128,16,128]{3,2,0,1:T(8,128)}, u32[]{:S(2)}, u32[]{:S(2)}) async-start(f32[1,128,16,128]{3,2,0,1:T(8,128)} %copy.173), calls=%async_computation.4 | async-start | bytes 2097152 | tf_op jit(solution)/shard_map/all_to_all | solution.py:76
  339.5 1.6 copy.168
  342.5 2.3 fusion.48
  344.8 17.5 %all-to-all-done.3 = f32[1,128,16,128]{3,2,0,1:T(8,128)} async-done(((f32[1,128,16,128]{3,2,0,1:T(8,128)}), f32[1,128,16,128]{3,2,0,1:T(8,128)}, u32[]{:S(2)}, u32[]{:S(2)}) %all-to-all-start.3) | async-done | bytes 1048608 | tf_op jit(solution)/shard_map/all_to_all | solution.py:76
  362.3 4.2 %all-to-all-start.2 = ((f32[1,128,16,128]{3,2,0,1:T(8,128)}), f32[1,128,16,128]{3,2,0,1:T(8,128)}, u32[]{:S(2)}, u32[]{:S(2)}) async-start(f32[1,128,16,128]{3,2,0,1:T(8,128)} %copy.168), calls=%async_computation.3 | async-start | bytes 2097152 | tf_op jit(solution)/shard_map/all_to_all | solution.py:75
  376.8 15.1 %all-to-all-done.2 = f32[1,128,16,128]{3,2,0,1:T(8,128)} async-done(((f32[1,128,16,128]{3,2,0,1:T(8,128)}), f32[1,128,16,128]{3,2,0,1:T(8,128)}, u32[]{:S(2)}, u32[]{:S(2)}) %all-to-all-start.2) | async-done | bytes 1048608 | tf_op jit(solution)/shard_map/all_to_all | solution.py:75
  403.6 4.5 %multiply_add_fusion = f32[1,16,128,128]{3,0,2,1:T(1,128)} fusion(f32[1,16,128,128]{3,0,2,1:T(1,128)S(1)} %bitcast.316, f32[1,16,128,128]{3,0,2,1:T(1,128)S(1)} %bitcast.315, f32[1,16,128,128]{3,0,2,1:T(1,128)S(1)} %bitcast.317, f32[1,16,128,128]{3,0,2,1:T(1,128)S(1)} %bitcast.318, f32[4,16,128,128]{3,0,2,1:T(4,128)S(1)} %copy-done.1), kind=kLoop, calls=%fused_computation.49 | loop fusion | flops 1835008 | bytes 9437184 | tf_op jit(solution)/shard_map/add | solution.py:159
  (109 shorter events, 80.8 us)
Async XLA Ops:
  7.2 84.3 %reduce-scatter.2.cloned.1.call-start = ((), (), s32[]{:S(2)}) async-start(), calls=%async_computation.9 | async-start | bytes 5242880 | tf_op jit(solution)/shard_map/reduce_scatter | solution.py:131
  49.3 78.9 %all-gather.4.cloned.1.call-start = ((), (), s32[]{:S(2)}) async-start(), calls=%async_computation.10 | async-start | bytes 5242880 | tf_op jit(solution)/shard_map/all_gather | solution.py:151
  92.6 44.1 %copy-start.3 = (f32[1,16,128,128]{3,2,1,0:T(8,128)S(1)}, f32[1,16,128,128]{3,2,1,0:T(8,128)}, u32[]{:S(2)}) copy-start(f32[1,16,128,128]{3,2,1,0:T(8,128)} %reduce-scatter.2.cloned.1.call-done) | copy-start | bytes 3145732
  136.7 3.6 copy-start
  145.2 1.0 copy-start.2
  150.4 32.0 %all-to-all-start.4 = ((f32[1,16,128,128]{3,1,0,2:T(8,128)}), f32[1,16,128,128]{3,1,0,2:T(8,128)}, u32[]{:S(2)}, u32[]{:S(2)}) async-start(f32[1,16,128,128]{3,1,0,2:T(8,128)} %copy.182), calls=%async_computation.5 | async-start | bytes 2097152 | tf_op jit(solution)/shard_map/all_to_all | solution.py:59
  182.4 29.9 %all-to-all-start.5 = ((f32[1,16,128,128]{3,1,0,2:T(8,128)}), f32[1,16,128,128]{3,1,0,2:T(8,128)}, u32[]{:S(2)}, u32[]{:S(2)}) async-start(f32[1,16,128,128]{3,1,0,2:T(8,128)} %copy.187), calls=%async_computation.6 | async-start | bytes 2097152 | tf_op jit(solution)/shard_map/all_to_all | solution.py:60
  212.2 29.7 %all-to-all-start.1 = ((f32[1,16,128,128]{3,1,0,2:T(8,128)}), f32[1,16,128,128]{3,1,0,2:T(8,128)S(1)}, u32[]{:S(2)}, u32[]{:S(2)}) async-start(f32[1,16,128,128]{3,1,0,2:T(8,128)} %copy.161), calls=%async_computation.2 | async-start | bytes 2097152 | tf_op jit(solution)/shard_map/all_to_all | solution.py:60
  242.0 7.7 %copy-start.5 = (f32[1,16,128,128]{3,1,0,2:T(8,128)}, f32[1,16,128,128]{3,1,0,2:T(8,128)S(1)}, u32[]{:S(2)}) copy-start(f32[1,16,128,128]{3,1,0,2:T(8,128)S(1)} %all-to-all-done.1) | copy-start | bytes 3145732
  242.0 29.6 %all-to-all-start = ((f32[1,16,128,128]{3,1,0,2:T(8,128)}), f32[1,16,128,128]{3,1,0,2:T(8,128)S(1)}, u32[]{:S(2)}, u32[]{:S(2)}) async-start(f32[1,16,128,128]{3,1,0,2:T(8,128)} %copy.156), calls=%async_computation.1 | async-start | bytes 2097152 | tf_op jit(solution)/shard_map/all_to_all | solution.py:59
  271.6 1.0 copy-start.7
  272.6 29.8 %all-to-all-start.6 = ((f32[1,128,16,128]{3,2,0,1:T(8,128)}), f32[1,128,16,128]{3,2,0,1:T(8,128)S(1)}, u32[]{:S(2)}, u32[]{:S(2)}) async-start(f32[1,128,16,128]{3,2,0,1:T(8,128)} %copy.194), calls=%async_computation.7 | async-start | bytes 2097152 | tf_op jit(solution)/shard_map/all_to_all | solution.py:75
  277.7 28.9 %copy-start.6 = (f32[1,16,128,128]{3,1,0,2:T(8,128)S(1)}, f32[1,16,128,128]{3,1,0,2:T(8,128)}, u32[]{:S(2)}) copy-start(f32[1,16,128,128]{3,1,0,2:T(8,128)} %copy-done.5) | copy-start | bytes 3145732
  279.0 27.7 %copy-start.8 = (f32[1,16,128,128]{3,1,0,2:T(8,128)S(1)}, f32[1,16,128,128]{3,1,0,2:T(8,128)}, u32[]{:S(2)}) copy-start(f32[1,16,128,128]{3,1,0,2:T(8,128)} %copy-done.7) | copy-start | bytes 3145732
  302.3 29.9 %all-to-all-start.7 = ((f32[1,128,16,128]{3,2,0,1:T(8,128)}), f32[1,128,16,128]{3,2,0,1:T(8,128)}, u32[]{:S(2)}, u32[]{:S(2)}) async-start(f32[1,128,16,128]{3,2,0,1:T(8,128)} %copy.199), calls=%async_computation.8 | async-start | bytes 2097152 | tf_op jit(solution)/shard_map/all_to_all | solution.py:76
  332.2 30.1 %all-to-all-start.3 = ((f32[1,128,16,128]{3,2,0,1:T(8,128)}), f32[1,128,16,128]{3,2,0,1:T(8,128)}, u32[]{:S(2)}, u32[]{:S(2)}) async-start(f32[1,128,16,128]{3,2,0,1:T(8,128)} %copy.173), calls=%async_computation.4 | async-start | bytes 2097152 | tf_op jit(solution)/shard_map/all_to_all | solution.py:76
  362.3 29.7 %all-to-all-start.2 = ((f32[1,128,16,128]{3,2,0,1:T(8,128)}), f32[1,128,16,128]{3,2,0,1:T(8,128)}, u32[]{:S(2)}, u32[]{:S(2)}) async-start(f32[1,128,16,128]{3,2,0,1:T(8,128)} %copy.168), calls=%async_computation.3 | async-start | bytes 2097152 | tf_op jit(solution)/shard_map/all_to_all | solution.py:75
  367.9 4.0 copy-start.4
  399.9 3.7 copy-start.1
Sparse Core Ops, SparseCore 0:
  49.4 41.9 reduce-scatter.1
  93.6 34.4 all-gather.3
